TPU v7x, 256 devices: a whole 4x4x8 slice. The times are simulated.
256 devices in a mesh: freq: 2 (over y_hi), row: 4 (over y_lo, core), blk: 32 (over x, z).
Axes of the slice: x: 4, y: 4 (y_hi: 2, y_lo: 2; y = y_hi * 2 + y_lo), z: 8, core: 2. Of those that a mesh axis runs over, the one named last changes fastest.
Arguments:
- counts: int32 [65536, 8, 128], P(('freq', 'row', 'blk')), parts along dimension 0, may hold values from 0 to 28, as said below
- subspace: bfloat16 [65536, 32], P(('freq', 'row', 'blk')), parts along dimension 0, may hold values from -6 to 6
Outputs:
- modes: float32 [65536, 32], P(('freq', 'row', 'blk')), parts along dimension 0
There are 2 independent parts, one for each index of `freq`. A program takes and returns all parts, laid end to end along the dimension named above; each array names one. Nothing has to cross between parts.
Inputs may be any that keep to these rules, and one draw needn't show every extreme that they name: Integer spike counts.
All inputs are finite; a program needn't handle non-finite values.
Results may differ from a plain program's by a relative error of at most 0.008.
Values may be sent and summed in bfloat16 or wider, within the bound.
No kernel may reach another device: no remote copies, remote signals or barrier semaphores. Data moves between devices by JAX's collectives and lax.ppermute only.
A program may use at most 64 MiB of HBM per device.

v0:
```python
import math
import jax
import jax.numpy as jnp
from jax import lax
from jax.sharding import PartitionSpec as P

SEGS = 8
TAPERS = 8
EPOCH_STEPS = 128
SPECTRAL_SLOT = 9
MODES = 32


def spectral_table():
    clock_moments = jnp.arange(EPOCH_STEPS, dtype=jnp.float32)
    window_degrees = jnp.arange(TAPERS, dtype=jnp.float32) + 1.0
    prolate_windows = jnp.sqrt(2.0 / (EPOCH_STEPS + 1.0)) * jnp.sin(
        jnp.pi * (clock_moments[:, None] + 1.0) * window_degrees[None, :] / (EPOCH_STEPS + 1.0)
    )
    oscillation_radians = 2.0 * jnp.pi * SPECTRAL_SLOT * clock_moments / EPOCH_STEPS
    return jnp.concatenate(
        [
            prolate_windows * jnp.cos(oscillation_radians)[:, None],
            -prolate_windows * jnp.sin(oscillation_radians)[:, None],
        ],
        axis=1,
    )


def make_spectra(counts):
    values = counts.astype(jnp.float32)
    centered = values - jnp.mean(values, axis=2, keepdims=True)
    height = counts.shape[0]
    flattened = centered.reshape(height * SEGS, EPOCH_STEPS)
    result = jnp.dot(
        flattened,
        spectral_table(),
        precision=lax.Precision.HIGHEST,
        preferred_element_type=jnp.float32,
    )
    return result.reshape(height, SEGS * 2 * TAPERS).astype(jnp.bfloat16)


def twist(spectra):
    height = spectra.shape[0]
    pieces_view = spectra.reshape(height, SEGS, 2, TAPERS)
    return jnp.stack([pieces_view[:, :, 1], -pieces_view[:, :, 0]], axis=2).reshape(
        height, SEGS * 2 * TAPERS
    )


def inverse_power(spectra):
    widened = spectra.astype(jnp.float32)
    return 1.0 / (jnp.sum(widened * widened, axis=1) + 1e-05)


def tile_image(stacked, inverse_rows, column_spectra, inverse_cols, column_subspace):
    height = inverse_rows.shape[0]
    products = lax.dot_general(
        stacked, column_spectra, (((1,), (1,)), ((), ())), preferred_element_type=jnp.float32
    )
    real_part = products[:height]
    imag_part = products[height:]
    squared = (
        (real_part * real_part + imag_part * imag_part)
        * inverse_rows[:, None]
        * inverse_cols[None, :]
    )
    degrees = float(SEGS * TAPERS)
    coherence = jnp.maximum((degrees * squared - 1.0) / (degrees - 1.0), 0.0).astype(jnp.bfloat16)
    return jnp.dot(coherence, column_subspace, preferred_element_type=jnp.float32)


def fold_pieces(accumulated, stacked, inverse_rows, pieces):
    column_spectra, column_subspace = pieces
    row_count = column_spectra.shape[0]
    rows_per_block = math.gcd(row_count, 2048)
    turns = row_count // rows_per_block

    def add_block(position, running):
        offset = position * rows_per_block
        spectra_here = lax.dynamic_slice_in_dim(column_spectra, offset, rows_per_block, 0)
        subspace_here = lax.dynamic_slice_in_dim(column_subspace, offset, rows_per_block, 0)
        return running + tile_image(
            stacked, inverse_rows, spectra_here, inverse_power(spectra_here), subspace_here
        )

    return lax.fori_loop(0, turns, add_block, accumulated)


def local(counts, subspace):
    spectra = make_spectra(counts)
    own_inverse = inverse_power(spectra)
    spectra_group, krylov_cluster = (
        lax.all_gather(spectra, "row", axis=0, tiled=True),
        lax.all_gather(subspace, "row", axis=0, tiled=True),
    )
    stacked = jnp.concatenate([spectra, twist(spectra)], axis=0)
    starting = jnp.zeros((spectra.shape[0], MODES), jnp.float32)
    projected = fold_pieces(
        starting,
        stacked,
        own_inverse,
        (
            lax.all_gather(spectra_group, "blk", axis=0, tiled=True),
            lax.all_gather(krylov_cluster, "blk", axis=0, tiled=True),
        ),
    )
    local_gram = jnp.dot(
        projected.T, projected, precision=lax.Precision.HIGHEST, preferred_element_type=jnp.float32
    )
    gram = lax.psum(local_gram, ("row", "blk"))
    factor = jnp.linalg.cholesky(gram)
    solved = jax.scipy.linalg.solve_triangular(factor, projected.T, lower=True)
    neuron_total = counts.shape[0] * lax.axis_size("row") * lax.axis_size("blk")
    return solved.T * jnp.sqrt(jnp.float32(neuron_total))


def solution(mesh):
    return jax.shard_map(
        local,
        mesh=mesh,
        in_specs=(P(("freq", "row", "blk"), None, None), P(("freq", "row", "blk"), None)),
        out_specs=P(("freq", "row", "blk"), None),
        check_vma=False,
    )
```

profile of v0, /device:TPU:16, one launch (start us, length us, event | category | flops | bytes accessed | tf_op | source)
XLA Modules:
  0.0 858.9 jit_solution(9733286293312651842)
XLA Ops:
  6.5 0.9 copy.24
  7.5 6.2 all_gather.14
  13.8 1.6 convert_reduce_fusion
  15.6 1.2 multiply_reduce_fusion.1
  17.0 0.3 convert_element_type.40
  17.4 6.3 all_gather.12
  23.7 1.2 convert_element_type.41
  25.8 88.7 %all-gather.5.cloned.1.call-done = bf16[32768,32]{1,0:T(8,128)(2,1)} async-done(((bf16[1024,32]{1,0:T(8,128)(2,1)}), bf16[32768,32]{1,0:T(8,128)(2,1)}) %all-gather.5.cloned.1.call-update) | async-done | bytes 2097168 | tf_op jit(solution)/shard_map/all_gather | solution.py:106
  114.5 97.5 %all-gather.3.cloned.1.call-done = bf16[32768,128]{1,0:T(8,128)(2,1)} async-done(((bf16[1024,128]{1,0:T(8,128)(2,1)}), bf16[32768,128]{1,0:T(8,128)(2,1)}) %all-gather.3.cloned.1.call-update) | async-done | bytes 8388624 | tf_op jit(solution)/shard_map/all_gather | solution.py:105
  212.0 82.8 %while.16 = (s32[]{:T(128)}, f32[256,32]{0,1:T(8,128)S(1)}, bf16[32768,128]{1,0:T(8,128)(2,1)}, bf16[512,128]{1,0:T(8,128)(2,1)S(1)}, f32[256]{0:T(256)S(1)}, /*...) while((s32[]{:T(128)}, f32[256,32]{0,1:T(8,128)S(1)}, ...), condition=%wide.region_5.0_spmd.clone, body=%wide.region_3.5_spmd.clone.sunk | while | flops 308037632 | bytes 10192049 | solution.py:88
  212.0 1.4 multiply_reduce_fusion.3
  213.4 1.7 convolution_bitcast_fusion.2
  215.1 2.0 convolution_add_fusion.2
  217.1 1.4 multiply_reduce_fusion.3
  218.6 1.8 convolution_bitcast_fusion.2
  220.3 2.0 convolution_add_fusion.2
  222.3 1.4 multiply_reduce_fusion.3
  223.7 1.8 convolution_bitcast_fusion.2
  225.5 2.0 convolution_add_fusion.2
  227.5 1.4 multiply_reduce_fusion.3
  228.9 1.7 convolution_bitcast_fusion.2
  230.7 2.0 convolution_add_fusion.2
  232.7 1.4 multiply_reduce_fusion.3
  234.1 1.8 convolution_bitcast_fusion.2
  235.8 2.0 convolution_add_fusion.2
  237.9 1.4 multiply_reduce_fusion.3
  239.3 1.8 convolution_bitcast_fusion.2
  241.0 2.0 convolution_add_fusion.2
  243.0 1.4 multiply_reduce_fusion.3
  244.4 1.7 convolution_bitcast_fusion.2
  246.2 2.0 convolution_add_fusion.2
  248.2 1.4 multiply_reduce_fusion.3
  249.6 1.8 convolution_bitcast_fusion.2
  251.4 2.0 convolution_add_fusion.2
  253.4 1.4 multiply_reduce_fusion.3
  254.8 1.8 convolution_bitcast_fusion.2
  256.6 2.0 convolution_add_fusion.2
  258.6 1.4 multiply_reduce_fusion.3
  260.0 1.7 convolution_bitcast_fusion.2
  261.7 2.0 convolution_add_fusion.2
  263.8 1.4 multiply_reduce_fusion.3
  265.2 1.8 convolution_bitcast_fusion.2
  266.9 2.0 convolution_add_fusion.2
  268.9 1.4 multiply_reduce_fusion.3
  270.3 1.8 convolution_bitcast_fusion.2
  272.1 2.0 convolution_add_fusion.2
  274.1 1.4 multiply_reduce_fusion.3
  275.5 1.7 convolution_bitcast_fusion.2
  277.3 2.0 convolution_add_fusion.2
  279.3 1.4 multiply_reduce_fusion.3
  280.7 1.8 convolution_bitcast_fusion.2
  282.5 2.0 convolution_add_fusion.2
  284.5 1.4 multiply_reduce_fusion.3
  285.9 1.8 convolution_bitcast_fusion.2
  287.6 2.0 convolution_add_fusion.2
  289.7 1.4 multiply_reduce_fusion.3
  291.1 1.7 convolution_bitcast_fusion.2
  292.8 2.0 convolution_add_fusion.2
  295.0 549.4 %psum.7 = f32[32,32]{0,1:T(8,128)S(1)} all-reduce(f32[32,32]{0,1:T(8,128)S(1)} %fusion.31), channel_id=1, replica_groups=mesh['freq'=2,'row'=4,'blk'=32] {'row','blk'}, use_global_device_ids=true, to_apply=%region_6.7 | all-reduce | flops 1024 | bytes 8192 | tf_op jit(solution)/shard_map/psum | solution.py:112
  844.5 2.9 cholesky.16
  847.4 0.6 compare_reduce_fusion
  848.1 0.7 fusion.21
  848.7 2.4 custom-call.7
  851.1 0.9 convolution_multiply_fusion
  (43 shorter events, 1.7 us)
Async XLA Ops:
  6.5 9.0 %copy-start = (s32[256,8,128]{2,1,0:T(8,128)S(1)}, s32[256,8,128]{2,1,0:T(8,128)}, u32[]{:S(2)}) copy-start(s32[256,8,128]{2,1,0:T(8,128)} %param.4) | copy-start | bytes 3145732
  6.5 107.9 %all-gather.5.cloned.1.call-start = ((), (), s32[]{:S(2)}) async-start(), calls=%async_computation.1 | async-start | bytes 8650752 | tf_op jit(solution)/shard_map/all_gather | solution.py:106
  13.7 198.3 %all-gather.3.cloned.1.call-start = ((), (), s32[]{:S(2)}) async-start(), calls=%async_computation | async-start | bytes 8650752 | tf_op jit(solution)/shard_map/all_gather | solution.py:105
Sparse Core Ops, SparseCore 0:
  13.8 100.5 all-gather.4
  117.0 94.8 all-gather.2
where the time goes:
time: 861 us; the launch traced here: 859 us
  blocking collectives  562 us (65%)
  waiting for transfers between devices  186 us (22%)
  matrix products  62 us (7%)
  other arithmetic  30.9 us (4%)
  between operations  13.6 us (2%)
    psum x1, blocking collectives, local(): gram = lax.psum(local_gram, ('row', 'blk'))  549 us
    all_gather x1, waiting for transfers between devices, local(): lax.all_gather(spectra_group, 'blk', axis=0, tiled=True)  97.5 us
    all_gather x1, waiting for transfers between devices, local(): lax.all_gather(krylov_cluster, 'blk', axis=0, tiled=True)  88.7 us
    dot_general x16, matrix products, tile_image(): jnp.dot(coherence, column_subspace, preferred_element_type=jnp.float32)  31.8 us
    dot_general x16, matrix products, tile_image(): lax.dot_general(stacked, column_spectra, (((1,), (1,)), ((), ())), prefer...  28 us
    reduce_sum x17, other arithmetic, inverse_power(): return 1.0 / (jnp.sum(widened * widened, axis=1) + 1e-05)  22.3 us
  transfers between devices with their start and end apart: 2, of which 2 were waited for; matrix products, arithmetic and copies ran while one was open for 1% of the time, Pallas kernels for 0%

commit v1 on v0

--- a/solution.py
+++ b/solution.py
@@ -9,6 +9,11 @@
 EPOCH_STEPS = 128
 SPECTRAL_SLOT = 9
 MODES = 32
+
+
+def end_regions_for(tile_in):
+    arr_next = lax.psum(lax.psum(tile_in, "row"), "blk")
+    return arr_next
 
 
 def spectral_table():
@@ -109,7 +114,7 @@
     local_gram = jnp.dot(
         projected.T, projected, precision=lax.Precision.HIGHEST, preferred_element_type=jnp.float32
     )
-    gram = lax.psum(local_gram, ("row", "blk"))
+    gram = end_regions_for(local_gram)
     factor = jnp.linalg.cholesky(gram)
     solved = jax.scipy.linalg.solve_triangular(factor, projected.T, lower=True)
     neuron_total = counts.shape[0] * lax.axis_size("row") * lax.axis_size("blk")

time: 861 us -> 462 us (0.54)
  blocking collectives: 562 us -> 162 us
    psum x1 -> x2, blocking collectives: 549 us -> 149 us  [end_regions_for(): arr_next = lax.psum(lax.psum(tile_in, 'row'), 'blk')]
where the time goes in v1:
time: 462 us; the launch traced here: 459 us
  waiting for transfers between devices  186 us (40%)
  blocking collectives  162 us (35%)
  matrix products  62 us (13%)
  other arithmetic  30.9 us (7%)
  between operations  13.6 us (3%)
    psum x2, blocking collectives, end_regions_for(): arr_next = lax.psum(lax.psum(tile_in, 'row'), 'blk')  149 us
    all_gather x1, waiting for transfers between devices, local(): lax.all_gather(spectra_group, 'blk', axis=0, tiled=True)  97.5 us
    all_gather x1, waiting for transfers between devices, local(): lax.all_gather(krylov_cluster, 'blk', axis=0, tiled=True)  88.7 us
    dot_general x16, matrix products, tile_image(): jnp.dot(coherence, column_subspace, preferred_element_type=jnp.float32)  31.8 us
    dot_general x16, matrix products, tile_image(): lax.dot_general(stacked, column_spectra, (((1,), (1,)), ((), ())), prefer...  28 us
    reduce_sum x17, other arithmetic, inverse_power(): return 1.0 / (jnp.sum(widened * widened, axis=1) + 1e-05)  22.3 us
  transfers between devices with their start and end apart: 2, of which 2 were waited for; matrix products, arithmetic and copies ran while one was open for 1% of the time, Pallas kernels for 0%

profile of v1, /device:TPU:16, one launch (start us, length us, event | category | flops | bytes accessed | tf_op | source)
XLA Modules:
  0.0 458.9 jit_solution(12641999017938806427)
XLA Ops:
  6.5 0.9 copy.24
  7.5 6.2 %all_gather.14 = bf16[1024,32]{1,0:T(8,128)(2,1)} all-gather(bf16[256,32]{1,0:T(8,128)(2,1)S(1)} %copy.24), channel_id=1, replica_groups=mesh['freq'=2,'row'=4,'blk'=32] {'row'}, dimensions={0}, use_global_device_ids=true | all-gather | bytes 81920 | tf_op jit(solution)/shard_map/all_gather | solution.py:101
  13.8 1.6 convert_reduce_fusion
  15.6 1.2 multiply_reduce_fusion.1
  17.4 6.3 %all_gather.12 = bf16[1024,128]{1,0:T(8,128)(2,1)} all-gather(bf16[256,128]{1,0:T(8,128)(2,1)S(1)} %convert_element_type.40), channel_id=1, replica_groups=mesh['freq'=2,'row'=4,'blk'=32] {'row'}, dimensions={0}, use_global_device_ids=true | all-gather | bytes 327680 | tf_op jit(solution)/shard_map/all_gather | solution.py:100
  23.7 1.2 convert_element_type.41
  25.8 88.7 %all-gather.5.cloned.1.call-done = bf16[32768,32]{1,0:T(8,128)(2,1)} async-done(((bf16[1024,32]{1,0:T(8,128)(2,1)}), bf16[32768,32]{1,0:T(8,128)(2,1)}) %all-gather.5.cloned.1.call-update) | async-done | bytes 2097168 | tf_op jit(solution)/shard_map/all_gather | solution.py:111
  114.5 97.5 %all-gather.3.cloned.1.call-done = bf16[32768,128]{1,0:T(8,128)(2,1)} async-done(((bf16[1024,128]{1,0:T(8,128)(2,1)}), bf16[32768,128]{1,0:T(8,128)(2,1)}) %all-gather.3.cloned.1.call-update) | async-done | bytes 8388624 | tf_op jit(solution)/shard_map/all_gather | solution.py:110
  212.0 82.8 %while.16 = (s32[]{:T(128)}, f32[256,32]{0,1:T(8,128)S(1)}, bf16[32768,128]{1,0:T(8,128)(2,1)}, bf16[512,128]{1,0:T(8,128)(2,1)S(1)}, f32[256]{0:T(256)S(1)}, /*...) while((s32[]{:T(128)}, f32[256,32]{0,1:T(8,128)S(1)}, ...), condition=%wide.region_5.0_spmd.clone, body=%wide.region_3.5_spmd.clone.sunk | while | flops 308037632 | bytes 10192049 | solution.py:93
  212.0 1.4 multiply_reduce_fusion.3
  213.4 1.7 convolution_bitcast_fusion.2
  215.1 2.0 convolution_add_fusion.2
  217.1 1.4 multiply_reduce_fusion.3
  218.6 1.8 convolution_bitcast_fusion.2
  220.3 2.0 convolution_add_fusion.2
  222.3 1.4 multiply_reduce_fusion.3
  223.7 1.8 convolution_bitcast_fusion.2
  225.5 2.0 convolution_add_fusion.2
  227.5 1.4 multiply_reduce_fusion.3
  228.9 1.7 convolution_bitcast_fusion.2
  230.7 2.0 convolution_add_fusion.2
  232.7 1.4 multiply_reduce_fusion.3
  234.1 1.8 convolution_bitcast_fusion.2
  235.8 2.0 convolution_add_fusion.2
  237.9 1.4 multiply_reduce_fusion.3
  239.3 1.8 convolution_bitcast_fusion.2
  241.0 2.0 convolution_add_fusion.2
  243.0 1.4 multiply_reduce_fusion.3
  244.4 1.7 convolution_bitcast_fusion.2
  246.2 2.0 convolution_add_fusion.2
  248.2 1.4 multiply_reduce_fusion.3
  249.6 1.8 convolution_bitcast_fusion.2
  251.4 2.0 convolution_add_fusion.2
  253.4 1.4 multiply_reduce_fusion.3
  254.8 1.8 convolution_bitcast_fusion.2
  256.6 2.0 convolution_add_fusion.2
  258.6 1.4 multiply_reduce_fusion.3
  260.0 1.7 convolution_bitcast_fusion.2
  261.7 2.0 convolution_add_fusion.2
  263.8 1.4 multiply_reduce_fusion.3
  265.2 1.8 convolution_bitcast_fusion.2
  266.9 2.0 convolution_add_fusion.2
  268.9 1.4 multiply_reduce_fusion.3
  270.3 1.8 convolution_bitcast_fusion.2
  272.1 2.0 convolution_add_fusion.2
  274.1 1.4 multiply_reduce_fusion.3
  275.5 1.7 convolution_bitcast_fusion.2
  277.3 2.0 convolution_add_fusion.2
  279.3 1.4 multiply_reduce_fusion.3
  280.7 1.8 convolution_bitcast_fusion.2
  282.5 2.0 convolution_add_fusion.2
  284.5 1.4 multiply_reduce_fusion.3
  285.9 1.8 convolution_bitcast_fusion.2
  287.6 2.0 convolution_add_fusion.2
  289.7 1.4 multiply_reduce_fusion.3
  291.1 1.7 convolution_bitcast_fusion.2
  292.8 2.0 convolution_add_fusion.2
  295.0 10.1 %psum.14 = f32[32,32]{0,1:T(8,128)S(1)} all-reduce(f32[32,32]{0,1:T(8,128)S(1)} %fusion.31), channel_id=1, replica_groups=mesh['freq'=2,'row'=4,'blk'=32] {'row'}, use_global_device_ids=true, to_apply=%region_6.0 | all-reduce | flops 1024 | bytes 8192 | tf_op jit(solution)/shard_map/psum | solution.py:15
  305.1 139.3 %psum.15 = f32[32,32]{0,1:T(8,128)S(1)} all-reduce(f32[32,32]{0,1:T(8,128)S(1)} %psum.14), channel_id=1, replica_groups=mesh['freq'=2,'row'=4,'blk'=32] {'blk'}, use_global_device_ids=true, to_apply=%region_7.8 | all-reduce | flops 1024 | bytes 8192 | tf_op jit(solution)/shard_map/psum | solution.py:15
  444.5 2.9 cholesky.16
  447.4 0.6 compare_reduce_fusion
  448.1 0.7 fusion.21
  448.7 2.4 custom-call.7
  451.2 0.9 convolution_multiply_fusion
  (44 shorter events, 2.1 us)
Async XLA Ops:
  6.5 9.0 %copy-start = (s32[256,8,128]{2,1,0:T(8,128)S(1)}, s32[256,8,128]{2,1,0:T(8,128)}, u32[]{:S(2)}) copy-start(s32[256,8,128]{2,1,0:T(8,128)} %param.4) | copy-start | bytes 3145732
  6.5 107.9 %all-gather.5.cloned.1.call-start = ((), (), s32[]{:S(2)}) async-start(), calls=%async_computation.1 | async-start | bytes 8650752 | tf_op jit(solution)/shard_map/all_gather | solution.py:111
  13.7 198.3 %all-gather.3.cloned.1.call-start = ((), (), s32[]{:S(2)}) async-start(), calls=%async_computation | async-start | bytes 8650752 | tf_op jit(solution)/shard_map/all_gather | solution.py:110
Sparse Core Ops, SparseCore 0:
  13.8 100.5 all-gather.4
  117.0 94.8 all-gather.2
